TPU v7x, 32 devices: a whole 2x2x4 slice. The times are simulated.
32 devices in a mesh: seq: 8 (over z, core), dp: 4 (over y, x).
Axes of the slice: x: 2, y: 2, z: 4, core: 2. Of those that a mesh axis runs over, the one named last changes fastest.
Arguments:
- query_proj: bfloat16 [3072, 2560], P(('dp', 'seq')), parts along dimension 0, may hold values from -4.5 to 4.5
- key_proj: bfloat16 [3072, 2560], P(('dp', 'seq')), parts along dimension 0, may hold values from -4.5 to 4.5
- value_proj: bfloat16 [3072, 2560], P(('dp', 'seq')), parts along dimension 0, may hold values from -16 to 16
- token_rows: int32 [3072], P('dp'), parts along dimension 0, may hold values from 0 to 767, as said below
- key_tiles: int32 [64, 4], P(('dp', 'seq')), parts along dimension 0, may hold values from 0 to 15, as said below
- key_count: int32 [64], P(('dp', 'seq')), parts along dimension 0, may hold values from 1 to 4
Outputs:
- attended: bfloat16 [3072, 2560], P(('dp', 'seq')), parts along dimension 0
There are 4 independent parts, one for each index of `dp`. A program takes and returns all parts, laid end to end along the dimension named above; each array names one. Nothing has to cross between parts.
Inputs may be any that keep to these rules, and one draw needn't show every extreme that they name: token_rows is a permutation; the rows of every aligned block of 96 frame-slab rows go to every aligned block of 96 tile-order rows exactly 96 // 8 times. `key_tiles`: for query tile i the entries m < key_count[i] are distinct, include i, and each lies between 2 * (i // 2 - 2) and 2 * (i // 2 + 2) + 1; later entries equal i.
All inputs are finite; a program needn't handle non-finite values.
Results may differ from a plain program's by a relative error of at most 0.0049.
Values may be sent and summed in bfloat16 or wider, within the bound.
No kernel may reach another device: no remote copies, remote signals or barrier semaphores. Data moves between devices by JAX's collectives and lax.ppermute only.
A program may use at most 64 MiB of HBM per device.

v0:
```python
import jax
import jax.numpy as jnp
from jax import lax
from jax.sharding import PartitionSpec as P

HD = 128
KMAX = 4
REACH = 2


def passed_along(value, axis, by):
    size = lax.axis_size(axis)
    pairs = [(i, i + by) for i in range(size) if 0 <= i + by < size]
    return lax.ppermute(value, axis, pairs)


def order_for(inverse, owner_dev, rows_dev):
    sources = lax.dynamic_slice_in_dim(inverse, owner_dev * rows_dev, rows_dev) // rows_dev
    keyed = sources * rows_dev + jnp.arange(rows_dev, dtype=jnp.int32)
    return jnp.argsort(keyed)


def attend_heads(query_rows, key_rows, value_rows, allowed, head_count):
    last = query_rows.ndim - 1

    def one_head(head_index):
        start = head_index * HD
        query_head = lax.dynamic_slice_in_dim(query_rows, start, HD, last)
        key_head = lax.dynamic_slice_in_dim(key_rows, start, HD, last)
        value_head = lax.dynamic_slice_in_dim(value_rows, start, HD, last)
        scores = jnp.einsum(
            "...qd,...kd->...qk", query_head, key_head, preferred_element_type=jnp.float32
        ) * HD ** (-0.5)
        scores = jnp.where(allowed, scores, -jnp.inf)
        peak = jnp.max(scores, axis=-1, keepdims=True)
        exponent = jnp.exp(scores - peak)
        weights = (exponent / jnp.sum(exponent, axis=-1, keepdims=True)).astype(jnp.bfloat16)
        mixed = jnp.einsum(
            "...qk,...kd->...qd", weights, value_head, preferred_element_type=jnp.float32
        )
        return mixed.astype(jnp.bfloat16)

    return lax.map(one_head, jnp.arange(head_count))


def shards(query_proj, key_proj, value_proj, token_rows, key_tiles, key_count):
    members = lax.axis_size("seq")
    myself = lax.axis_index("seq")
    rows_dev = query_proj.shape[0]
    feat_width = query_proj.shape[1]
    per_peer = rows_dev // members
    tile_rows = rows_dev // 2
    head_count = feat_width // HD
    inverse = jnp.argsort(token_rows)
    own_dest = lax.dynamic_slice_in_dim(token_rows, myself * rows_dev, rows_dev)
    send_order = jnp.argsort(own_dest)
    sorted_query = query_proj[send_order].reshape(members, per_peer, feat_width)
    sorted_keys = key_proj[send_order].reshape(members, per_peer, feat_width)
    sorted_values = value_proj[send_order].reshape(members, per_peer, feat_width)
    order_own = order_for(inverse, myself, rows_dev)
    placement_own = jnp.argsort(order_own)
    arrived_query, arrived_keys, arrived_values = (
        lax.all_to_all(sorted_query, "seq", split_axis=0, concat_axis=0, tiled=True),
        lax.all_to_all(sorted_keys, "seq", split_axis=0, concat_axis=0, tiled=True),
        lax.all_to_all(sorted_values, "seq", split_axis=0, concat_axis=0, tiled=True),
    )
    query_tile = arrived_query.reshape(rows_dev, feat_width)[placement_own]
    key_tile = arrived_keys.reshape(rows_dev, feat_width)[placement_own]
    value_tile = arrived_values.reshape(rows_dev, feat_width)[placement_own]
    blocks = []
    for offset in range(-REACH, REACH + 1):
        if offset == 0:
            blocks.append((key_tile, value_tile))
        else:
            blocks.append(passed_along((key_tile, value_tile), "seq", -offset))
    window_keys = jnp.concatenate([pair[0] for pair in blocks], axis=0)
    window_values = jnp.concatenate([pair[1] for pair in blocks], axis=0)
    entry_live = jnp.arange(KMAX)[None, :] < key_count[:, None]
    window_ids = (
        (myself + jnp.arange(-REACH, REACH + 1))[:, None] * 2 + jnp.arange(2)[None, :]
    ).reshape(-1)
    matches = (key_tiles[:, :, None] == window_ids[None, None, :]) & entry_live[:, :, None]
    listed = jnp.any(matches, axis=1)
    allowed = jnp.repeat(jnp.repeat(listed, tile_rows, axis=0), tile_rows, axis=1)
    mixed = attend_heads(query_tile, window_keys, window_values, allowed, head_count)
    tile_out = jnp.moveaxis(mixed, 0, -2).reshape(rows_dev, feat_width)
    back_send = tile_out[order_own].reshape(members, per_peer, feat_width)
    arrived_back = lax.all_to_all(back_send, "seq", split_axis=0, concat_axis=0, tiled=True)
    return arrived_back.reshape(rows_dev, feat_width)[jnp.argsort(send_order)]


def solution(mesh):
    return jax.shard_map(
        shards,
        mesh=mesh,
        in_specs=(
            P(("dp", "seq"), None),
            P(("dp", "seq"), None),
            P(("dp", "seq"), None),
            P("dp"),
            P(("dp", "seq"), None),
            P(("dp", "seq")),
        ),
        out_specs=P(("dp", "seq"), None),
        check_vma=False,
    )
```

profile of v0, /device:TPU:0, one launch (start us, length us, event | category | flops | bytes accessed | tf_op | source)
XLA Modules:
  0.0 226.7 jit_solution(4143252565832732605)
XLA Ops:
  0.0 5.1 %sort.77 = (s32[768]{0:T(1024)}, s32[768]{0:T(1024)S(1)}) sort(s32[768]{0:T(1024)} %param.11, s32[768]{0:T(1024)S(1)} %iota.41), dimensions={0}, to_apply=%region_1.2 | sort | flops 7680 | bytes 12288 | tf_op jit(solution)/shard_map/jit(argsort)/sort | solution.py:54
  6.0 2.5 %sort.78 = (s32[96]{0:T(128)}, s32[96]{0:T(128)S(1)}) sort(s32[96]{0:T(128)S(1)} %iota_add_fusion.1, s32[96]{0:T(128)S(1)} %iota.43), dimensions={0}, to_apply=%region_2.3 | sort | flops 672 | bytes 1536 | tf_op jit(solution)/shard_map/jit(argsort)/sort | solution.py:20
  8.5 2.5 %sort.76 = (s32[96]{0:T(128)}, s32[96]{0:T(128)S(1)}) sort(s32[96]{0:T(128)S(1)} %dynamic_slice.19, s32[96]{0:T(128)S(1)} %iota.40), dimensions={0}, to_apply=%region_0.0 | sort | flops 672 | bytes 1536 | tf_op jit(solution)/shard_map/jit(argsort)/sort | solution.py:56
  12.9 6.4 %all-to-all-start.2 = ((bf16[8,12,2560]{2,1,0:T(8,128)(2,1)}), bf16[8,12,2560]{2,1,0:T(8,128)(2,1)S(1)}, u32[]{:S(2)}, u32[]{:S(2)}) async-start(bf16[8,12,2560]{2,1,0:T(8,128)(2,1)} %reshape.86), calls=%async_computation.2 | async-start | bytes 1310720 | tf_op jit(solution)/shard_map/all_to_all | solution.py:65
  21.1 16.3 %all-to-all-done.2 = bf16[8,12,2560]{2,1,0:T(8,128)(2,1)S(1)} async-done(((bf16[8,12,2560]{2,1,0:T(8,128)(2,1)}), bf16[8,12,2560]{2,1,0:T(8,128)(2,1)S(1)}, u32[]{:S(2)}, u32[]{:S(2)}) %all-to-all-start.2) | async-done | bytes 491552 | tf_op jit(solution)/shard_map/all_to_all | solution.py:65
  37.4 3.5 %all-to-all-start.1 = ((bf16[8,12,2560]{2,1,0:T(8,128)(2,1)}), bf16[8,12,2560]{2,1,0:T(8,128)(2,1)S(1)}, u32[]{:S(2)}, u32[]{:S(2)}) async-start(bf16[8,12,2560]{2,1,0:T(8,128)(2,1)} %reshape.82), calls=%async_computation.1 | async-start | bytes 1310720 | tf_op jit(solution)/shard_map/all_to_all | solution.py:64
  40.9 2.5 %sort.79 = (s32[96]{0:T(128)}, s32[96]{0:T(128)S(1)}) sort(s32[96]{0:T(128)S(1)} %get-tuple-element.49, s32[96]{0:T(128)S(1)} %iota.44), dimensions={0}, to_apply=%region_3.4 | sort | flops 672 | bytes 1536 | tf_op jit(solution)/shard_map/jit(argsort)/sort | solution.py:61
  45.3 13.7 %all-to-all-done.1 = bf16[8,12,2560]{2,1,0:T(8,128)(2,1)S(1)} async-done(((bf16[8,12,2560]{2,1,0:T(8,128)(2,1)}), bf16[8,12,2560]{2,1,0:T(8,128)(2,1)S(1)}, u32[]{:S(2)}, u32[]{:S(2)}) %all-to-all-start.1) | async-done | bytes 491552 | tf_op jit(solution)/shard_map/all_to_all | solution.py:64
  59.0 3.5 %all-to-all-start = ((bf16[8,12,2560]{2,1,0:T(8,128)(2,1)}), bf16[8,12,2560]{2,1,0:T(8,128)(2,1)S(1)}, u32[]{:S(2)}, u32[]{:S(2)}) async-start(bf16[8,12,2560]{2,1,0:T(8,128)(2,1)} %reshape.80), calls=%async_computation | async-start | bytes 1310720 | tf_op jit(solution)/shard_map/all_to_all | solution.py:63
  63.6 4.6 %collective-permute-start.4 = (bf16[96,2560]{1,0:T(8,128)(2,1)S(1)}, bf16[96,2560]{1,0:T(8,128)(2,1)}, u32[]{:S(2)}, u32[]{:S(2)}) collective-permute-start(bf16[96,2560]{1,0:T(8,128)(2,1)S(1)} %gather_fusion.5), channel_id=1, source_target_pairs={{0,8},{4,12},{8,16},{12,20},{16,24},{20,28},{1,9},{5,13},{9,17},{1... | collective-permute-start | bytes 1474568 | tf_op jit(solution)/shard_map/ppermute | solution.py:14
  68.3 2.5 %collective-permute-start.5 = (bf16[96,2560]{1,0:T(8,128)(2,1)S(1)}, bf16[96,2560]{1,0:T(8,128)(2,1)}, u32[]{:S(2)}, u32[]{:S(2)}) collective-permute-start(bf16[96,2560]{1,0:T(8,128)(2,1)S(1)} %gather_fusion.5), channel_id=1, source_target_pairs={{0,4},{4,8},{8,12},{12,16},{16,20},{20,24},{24,28},{1,5},{5,9},{9,... | collective-permute-start | bytes 1474568 | tf_op jit(solution)/shard_map/ppermute | solution.py:14
  71.3 1.3 collective-permute-start.6
  72.6 1.3 collective-permute-start.7
  74.9 5.8 %collective-permute-start = (bf16[96,2560]{1,0:T(8,128)(2,1)S(1)}, bf16[96,2560]{1,0:T(8,128)(2,1)}, u32[]{:S(2)}, u32[]{:S(2)}) collective-permute-start(bf16[96,2560]{1,0:T(8,128)(2,1)S(1)} %gather_fusion.3), channel_id=1, source_target_pairs={{0,8},{4,12},{8,16},{12,20},{16,24},{20,28},{1,9},{5,13},{9,17},{1... | collective-permute-start | bytes 1474568 | tf_op jit(solution)/shard_map/ppermute | solution.py:14
  82.2 2.7 %collective-permute-done.4 = bf16[96,2560]{1,0:T(8,128)(2,1)} collective-permute-done((bf16[96,2560]{1,0:T(8,128)(2,1)S(1)}, bf16[96,2560]{1,0:T(8,128)(2,1)}, u32[]{:S(2)}, u32[]{:S(2)}) %collective-permute-start.4) | collective-permute-done | bytes 491552 | tf_op jit(solution)/shard_map/ppermute | solution.py:14
  84.9 1.6 collective-permute-start.1
  86.5 1.8 constant_dynamic-update-slice_fusion.9
  88.4 1.3 collective-permute-start.2
  89.6 1.9 constant_dynamic-update-slice_fusion.8
  92.3 3.1 %collective-permute-done = bf16[96,2560]{1,0:T(8,128)(2,1)} collective-permute-done((bf16[96,2560]{1,0:T(8,128)(2,1)S(1)}, bf16[96,2560]{1,0:T(8,128)(2,1)}, u32[]{:S(2)}, u32[]{:S(2)}) %collective-permute-start) | collective-permute-done | bytes 491552 | tf_op jit(solution)/shard_map/ppermute | solution.py:14
  95.5 1.3 collective-permute-start.3
  97.9 1.9 constant_dynamic-update-slice_fusion.6
  99.8 1.9 constant_dynamic-update-slice_fusion.5
  101.7 13.1 %collective-permute-done.3 = bf16[96,2560]{1,0:T(8,128)(2,1)S(1)} collective-permute-done((bf16[96,2560]{1,0:T(8,128)(2,1)S(1)}, bf16[96,2560]{1,0:T(8,128)(2,1)S(1)}, u32[]{:S(2)}, u32[]{:S(2)}) %collective-permute-start.3) | collective-permute-done | bytes 491552 | tf_op jit(solution)/shard_map/ppermute | solution.py:14
  114.8 1.4 copy-done.3
  116.3 79.9 %while.11 = (s32[]{:T(128)}, bf16[20,96,128]{2,1,0:T(8,128)(2,1)S(1)}, s32[20]{0:T(128)S(1)}, bf16[96,2560]{1,0:T(8,128)(2,1)S(1)}, bf16[480,2560]{1,0:T(8,128)(...) while((s32[]{:T(128)}, ...), condition=%wide.region_8.9_spmd.clone, body=%wide.region_5.8_spmd.clone.sunk | while | flops 23973700 | bytes 1052395 | solution.py:43
  117.7 1.2 fusion.20
  125.7 1.2 fusion.20
  129.7 1.2 fusion.20
  133.7 1.2 fusion.20
  137.7 1.2 fusion.20
  141.7 1.2 fusion.20
  145.7 1.2 fusion.20
  149.7 1.2 fusion.20
  153.7 1.2 fusion.20
  157.6 1.2 fusion.20
  161.6 1.2 fusion.20
  165.6 1.2 fusion.20
  169.6 1.2 fusion.20
  173.6 1.2 fusion.20
  177.6 1.2 fusion.20
  181.6 1.2 fusion.20
  189.6 1.2 fusion.20
  193.6 1.2 fusion.20
  198.1 8.8 %all-to-all-start.3 = ((bf16[8,12,2560]{2,1,0:T(8,128)(2,1)}), bf16[8,12,2560]{2,1,0:T(8,128)(2,1)S(1)}, u32[]{:S(2)}, u32[]{:S(2)}) async-start(bf16[8,12,2560]{2,1,0:T(8,128)(2,1)} %reshape.89), calls=%async_computation.3 | async-start | bytes 1310720 | tf_op jit(solution)/shard_map/all_to_all | solution.py:88
  206.8 2.5 %sort.80 = (s32[96]{0:T(128)}, s32[96]{0:T(128)S(1)}) sort(s32[96]{0:T(128)S(1)} %get-tuple-element.47, s32[96]{0:T(128)S(1)} %iota.46), dimensions={0}, to_apply=%region_9.10 | sort | flops 672 | bytes 1536 | tf_op jit(solution)/shard_map/jit(argsort)/sort | solution.py:89
  209.4 15.6 %all-to-all-done.3 = bf16[8,12,2560]{2,1,0:T(8,128)(2,1)S(1)} async-done(((bf16[8,12,2560]{2,1,0:T(8,128)(2,1)}), bf16[8,12,2560]{2,1,0:T(8,128)(2,1)S(1)}, u32[]{:S(2)}, u32[]{:S(2)}) %all-to-all-start.3) | async-done | bytes 491552 | tf_op jit(solution)/shard_map/all_to_all | solution.py:88
  225.1 1.6 gather_fusion.7
  (167 shorter events, 58.7 us)
Async XLA Ops:
  0.0 11.1 %copy-start = (bf16[96,2560]{1,0:T(8,128)(2,1)S(1)}, bf16[96,2560]{1,0:T(8,128)(2,1)}, u32[]{:S(2)}) copy-start(bf16[96,2560]{1,0:T(8,128)(2,1)} %param.10) | copy-start | bytes 1474564
  11.1 8.2 %copy-start.1 = (bf16[96,2560]{1,0:T(8,128)(2,1)S(1)}, bf16[96,2560]{1,0:T(8,128)(2,1)}, u32[]{:S(2)}) copy-start(bf16[96,2560]{1,0:T(8,128)(2,1)} %param.9) | copy-start | bytes 1474564
  12.9 24.5 %all-to-all-start.2 = ((bf16[8,12,2560]{2,1,0:T(8,128)(2,1)}), bf16[8,12,2560]{2,1,0:T(8,128)(2,1)S(1)}, u32[]{:S(2)}, u32[]{:S(2)}) async-start(bf16[8,12,2560]{2,1,0:T(8,128)(2,1)} %reshape.86), calls=%async_computation.2 | async-start | bytes 1310720 | tf_op jit(solution)/shard_map/all_to_all | solution.py:65
  19.3 24.2 %copy-start.2 = (bf16[96,2560]{1,0:T(8,128)(2,1)S(1)}, bf16[96,2560]{1,0:T(8,128)(2,1)}, u32[]{:S(2)}) copy-start(bf16[96,2560]{1,0:T(8,128)(2,1)} %param.8) | copy-start | bytes 1474564
  37.4 21.6 %all-to-all-start.1 = ((bf16[8,12,2560]{2,1,0:T(8,128)(2,1)}), bf16[8,12,2560]{2,1,0:T(8,128)(2,1)S(1)}, u32[]{:S(2)}, u32[]{:S(2)}) async-start(bf16[8,12,2560]{2,1,0:T(8,128)(2,1)} %reshape.82), calls=%async_computation.1 | async-start | bytes 1310720 | tf_op jit(solution)/shard_map/all_to_all | solution.py:64
  59.0 22.2 %all-to-all-start = ((bf16[8,12,2560]{2,1,0:T(8,128)(2,1)}), bf16[8,12,2560]{2,1,0:T(8,128)(2,1)S(1)}, u32[]{:S(2)}, u32[]{:S(2)}) async-start(bf16[8,12,2560]{2,1,0:T(8,128)(2,1)} %reshape.80), calls=%async_computation | async-start | bytes 1310720 | tf_op jit(solution)/shard_map/all_to_all | solution.py:63
  62.7 8.1 %copy-start.6 = (s32[2]{0:T(128)S(1)}, s32[2]{0:T(128)}, u32[]{:S(2)}) copy-start(s32[2]{0:T(128)} %param.13) | copy-start | bytes 28
  62.7 8.2 %copy-start.5 = (s32[2,4]{1,0:T(2,128)S(1)}, s32[2,4]{1,0:T(2,128)}, u32[]{:S(2)}) copy-start(s32[2,4]{1,0:T(2,128)} %param.12) | copy-start | bytes 100
  63.6 21.3 %collective-permute-start.4 = (bf16[96,2560]{1,0:T(8,128)(2,1)S(1)}, bf16[96,2560]{1,0:T(8,128)(2,1)}, u32[]{:S(2)}, u32[]{:S(2)}) collective-permute-start(bf16[96,2560]{1,0:T(8,128)(2,1)S(1)} %gather_fusion.5), channel_id=1, source_target_pairs={{0,8},{4,12},{8,16},{12,20},{16,24},{20,28},{1,9},{5,13},{9,17},{1... | collective-permute-start | bytes 1474568 | tf_op jit(solution)/shard_map/ppermute | solution.py:14
  68.3 20.1 %collective-permute-start.5 = (bf16[96,2560]{1,0:T(8,128)(2,1)S(1)}, bf16[96,2560]{1,0:T(8,128)(2,1)}, u32[]{:S(2)}, u32[]{:S(2)}) collective-permute-start(bf16[96,2560]{1,0:T(8,128)(2,1)S(1)} %gather_fusion.5), channel_id=1, source_target_pairs={{0,4},{4,8},{8,12},{12,16},{16,20},{20,24},{24,28},{1,5},{5,9},{9,... | collective-permute-start | bytes 1474568 | tf_op jit(solution)/shard_map/ppermute | solution.py:14
  71.3 26.6 %collective-permute-start.6 = (bf16[96,2560]{1,0:T(8,128)(2,1)S(1)}, bf16[96,2560]{1,0:T(8,128)(2,1)}, u32[]{:S(2)}, u32[]{:S(2)}) collective-permute-start(bf16[96,2560]{1,0:T(8,128)(2,1)S(1)} %gather_fusion.5), channel_id=1, source_target_pairs={{4,0},{8,4},{12,8},{16,12},{20,16},{24,20},{28,24},{5,1},{9,5},{13... | collective-permute-start | bytes 1474568 | tf_op jit(solution)/shard_map/ppermute | solution.py:14
  72.6 27.2 %collective-permute-start.7 = (bf16[96,2560]{1,0:T(8,128)(2,1)S(1)}, bf16[96,2560]{1,0:T(8,128)(2,1)}, u32[]{:S(2)}, u32[]{:S(2)}) collective-permute-start(bf16[96,2560]{1,0:T(8,128)(2,1)S(1)} %gather_fusion.5), channel_id=1, source_target_pairs={{8,0},{12,4},{16,8},{20,12},{24,16},{28,20},{9,1},{13,5},{17,9},{2... | collective-permute-start | bytes 1474568 | tf_op jit(solution)/shard_map/ppermute | solution.py:14
  74.9 20.6 %collective-permute-start = (bf16[96,2560]{1,0:T(8,128)(2,1)S(1)}, bf16[96,2560]{1,0:T(8,128)(2,1)}, u32[]{:S(2)}, u32[]{:S(2)}) collective-permute-start(bf16[96,2560]{1,0:T(8,128)(2,1)S(1)} %gather_fusion.3), channel_id=1, source_target_pairs={{0,8},{4,12},{8,16},{12,20},{16,24},{20,28},{1,9},{5,13},{9,17},{1... | collective-permute-start | bytes 1474568 | tf_op jit(solution)/shard_map/ppermute | solution.py:14
  84.9 12.9 %collective-permute-start.1 = (bf16[96,2560]{1,0:T(8,128)(2,1)S(1)}, bf16[96,2560]{1,0:T(8,128)(2,1)S(1)}, u32[]{:S(2)}, u32[]{:S(2)}) collective-permute-start(bf16[96,2560]{1,0:T(8,128)(2,1)S(1)} %gather_fusion.3), channel_id=1, source_target_pairs={{0,4},{4,8},{8,12},{12,16},{16,20},{20,24},{24,28},{1,5},{5,9},{9,... | collective-permute-start | bytes 1474568 | tf_op jit(solution)/shard_map/ppermute | solution.py:14
  88.4 13.3 %collective-permute-start.2 = (bf16[96,2560]{1,0:T(8,128)(2,1)S(1)}, bf16[96,2560]{1,0:T(8,128)(2,1)S(1)}, u32[]{:S(2)}, u32[]{:S(2)}) collective-permute-start(bf16[96,2560]{1,0:T(8,128)(2,1)S(1)} %gather_fusion.3), channel_id=1, source_target_pairs={{4,0},{8,4},{12,8},{16,12},{20,16},{24,20},{28,24},{5,1},{9,5},{13... | collective-permute-start | bytes 1474568 | tf_op jit(solution)/shard_map/ppermute | solution.py:14
  95.5 19.3 %collective-permute-start.3 = (bf16[96,2560]{1,0:T(8,128)(2,1)S(1)}, bf16[96,2560]{1,0:T(8,128)(2,1)S(1)}, u32[]{:S(2)}, u32[]{:S(2)}) collective-permute-start(bf16[96,2560]{1,0:T(8,128)(2,1)S(1)} %gather_fusion.3), channel_id=1, source_target_pairs={{8,0},{12,4},{16,8},{20,12},{24,16},{28,20},{9,1},{13,5},{17,9},{2... | collective-permute-start | bytes 1474568 | tf_op jit(solution)/shard_map/ppermute | solution.py:14
  97.9 18.4 %copy-start.4 = (bf16[20,96,128]{2,1,0:T(8,128)(2,1)S(1)}, bf16[20,96,128]{2,1,0:T(8,128)(2,1)}, u32[]{:S(2)}) copy-start(bf16[20,96,128]{2,1,0:T(8,128)(2,1)} %custom-call.18) | copy-start | bytes 1474564
  114.8 1.4 copy-start.3
  198.1 26.9 %all-to-all-start.3 = ((bf16[8,12,2560]{2,1,0:T(8,128)(2,1)}), bf16[8,12,2560]{2,1,0:T(8,128)(2,1)S(1)}, u32[]{:S(2)}, u32[]{:S(2)}) async-start(bf16[8,12,2560]{2,1,0:T(8,128)(2,1)} %reshape.89), calls=%async_computation.3 | async-start | bytes 1310720 | tf_op jit(solution)/shard_map/all_to_all | solution.py:88
where the time goes:
time: 229 us; the launch traced here: 227 us
  waiting for transfers between devices  65 us (28%)
  matrix products  47.2 us (21%)
  starting transfers between devices  41.8 us (18%)
  local copies, waits for them, and re-layouts  38.8 us (17%)
  other arithmetic  19.6 us (9%)
  loops' own time  14 us (6%)
    dot_general x20, matrix products, one_head(): jnp.einsum('...qd,...kd->...qk', query_head, key_head, preferred_element_...  24.2 us
    dot_general x20, matrix products, one_head(): jnp.einsum('...qk,...kd->...qd', weights, value_head, preferred_element_t...  23 us
    ppermute x8, starting transfers between devices, passed_along(): return lax.ppermute(value, axis, pairs)  19.6 us
    ppermute x8, waiting for transfers between devices, passed_along(): return lax.ppermute(value, axis, pairs)  18.9 us
    all_to_all x1, waiting for transfers between devices, shards(): lax.all_to_all(sorted_values, 'seq', split_axis=0, concat_axis=0, tiled=T...  16.3 us
    all_to_all x1, waiting for transfers between devices, shards(): lax.all_to_all(back_send, 'seq', split_axis=0, concat_axis=0, tiled=True)  15.6 us
    another operation x1, loops' own time, attend_heads(): return lax.map(one_head, jnp.arange(head_count))  14 us
    all_to_all x1, waiting for transfers between devices, shards(): lax.all_to_all(sorted_keys, 'seq', split_axis=0, concat_axis=0, tiled=True)  13.7 us
  transfers between devices with their start and end apart: 12, of which 7 were waited for; matrix products, arithmetic and copies ran while one was open for 10% of the time, Pallas kernels for 0%

commit v1 on v0

--- a/solution.py
+++ b/solution.py
@@ -6,6 +6,18 @@
 HD = 128
 KMAX = 4
 REACH = 2
+
+
+def sent_to_each(array, axis, split, join):
+    ways, here = (lax.axis_size(axis), lax.axis_index(axis))
+    width = array.shape[split] // ways
+    turned = jnp.roll(array, -here * width, axis=split)
+    got = [lax.slice_in_dim(turned, 0, width, axis=split)]
+    for far in range(1, ways):
+        sent = lax.slice_in_dim(turned, far * width, (far + 1) * width, axis=split)
+        got.append(lax.ppermute(sent, axis, [(d, (d + far) % ways) for d in range(ways)]))
+    line = jnp.concatenate(got[::-1], axis=join)
+    return jnp.roll(line, (here + 1) * got[0].shape[join], axis=join)
 
 
 def passed_along(value, axis, by):
@@ -62,7 +74,7 @@
     arrived_query, arrived_keys, arrived_values = (
         lax.all_to_all(sorted_query, "seq", split_axis=0, concat_axis=0, tiled=True),
         lax.all_to_all(sorted_keys, "seq", split_axis=0, concat_axis=0, tiled=True),
-        lax.all_to_all(sorted_values, "seq", split_axis=0, concat_axis=0, tiled=True),
+        sent_to_each(sorted_values, "seq", 0, 0),
     )
     query_tile = arrived_query.reshape(rows_dev, feat_width)[placement_own]
     key_tile = arrived_keys.reshape(rows_dev, feat_width)[placement_own]

time: 229 us -> 218 us (0.952)
  waiting for transfers between devices: 65 us -> 50.7 us
  starting transfers between devices: 41.8 us -> 44.4 us
    all_to_all x1 -> x0, waiting for transfers between devices: 16.3 us -> none  [shards(): lax.all_to_all(sorted_values, 'seq', split_axis=0, concat_axis=0, tiled=T...]
    all_to_all x1, waiting for transfers between devices: 13.7 us -> 0.01 us  [shards(): lax.all_to_all(sorted_keys, 'seq', split_axis=0, concat_axis=0, tiled=True)]
    ppermute x0 -> x7, waiting for transfers between devices: none -> 13.5 us  [sent_to_each(): lax.ppermute(sent, axis, [(d, (d + far) % ways) for d in range(ways)])]
    ppermute x0 -> x7, starting transfers between devices: none -> 10 us  [sent_to_each(): lax.ppermute(sent, axis, [(d, (d + far) % ways) for d in range(ways)])]
    all_to_all x1 -> x0, starting transfers between devices: 6.35 us -> none  [shards(): lax.all_to_all(sorted_values, 'seq', split_axis=0, concat_axis=0, tiled=T...]
    all_to_all x1, starting transfers between devices: 8.77 us -> 3.54 us  [shards(): lax.all_to_all(back_send, 'seq', split_axis=0, concat_axis=0, tiled=True)]
    all_to_all x1, waiting for transfers between devices: 0.53 us -> 4.64 us  [shards(): lax.all_to_all(sorted_query, 'seq', split_axis=0, concat_axis=0, tiled=True)]
    all_to_all x1, starting transfers between devices: 3.54 us -> 7.44 us  [shards(): lax.all_to_all(sorted_query, 'seq', split_axis=0, concat_axis=0, tiled=True)]
  transfers between devices with their start and end apart: 12 -> 18, of which waited for: 7 -> 8; matrix products, arithmetic and copies ran while one was open for 10% -> 10% of each run, Pallas kernels for 0% -> 0%
where the time goes in v1:
time: 218 us; the launch traced here: 216 us
  waiting for transfers between devices  50.7 us (23%)
  matrix products  47.2 us (22%)
  starting transfers between devices  44.4 us (20%)
  local copies, waits for them, and re-layouts  39.1 us (18%)
  other arithmetic  20.2 us (9%)
  loops' own time  14 us (6%)
    dot_general x20, matrix products, one_head(): jnp.einsum('...qd,...kd->...qk', query_head, key_head, preferred_element_...  24.2 us
    dot_general x20, matrix products, one_head(): jnp.einsum('...qk,...kd->...qd', weights, value_head, preferred_element_t...  23 us
    ppermute x8, starting transfers between devices, passed_along(): return lax.ppermute(value, axis, pairs)  18.6 us
    ppermute x8, waiting for transfers between devices, passed_along(): return lax.ppermute(value, axis, pairs)  17 us
    all_to_all x1, waiting for transfers between devices, shards(): lax.all_to_all(back_send, 'seq', split_axis=0, concat_axis=0, tiled=True)  15.5 us
    another operation x1, loops' own time, attend_heads(): return lax.map(one_head, jnp.arange(head_count))  14 us
    ppermute x7, waiting for transfers between devices, sent_to_each(): lax.ppermute(sent, axis, [(d, (d + far) % ways) for d in range(ways)])  13.5 us
    dynamic_slice x20, local copies, waits for them, and re-layouts, attend_heads(): return lax.map(one_head, jnp.arange(head_count))  11.7 us
  transfers between devices with their start and end apart: 18, of which 8 were waited for; matrix products, arithmetic and copies ran while one was open for 10% of the time, Pallas kernels for 0%

profile of v1, /device:TPU:0, one launch (start us, length us, event | category | flops | bytes accessed | tf_op | source)
XLA Modules:
  0.0 215.9 jit_solution(7567674167178901826)
XLA Ops:
  0.0 5.1 %sort.77 = (s32[768]{0:T(1024)}, s32[768]{0:T(1024)S(1)}) sort(s32[768]{0:T(1024)} %param.13, s32[768]{0:T(1024)S(1)} %iota.41), dimensions={0}, to_apply=%region_1.2 | sort | flops 7680 | bytes 12288 | tf_op jit(solution)/shard_map/jit(argsort)/sort | solution.py:66
  6.0 2.5 %sort.78 = (s32[96]{0:T(128)}, s32[96]{0:T(128)S(1)}) sort(s32[96]{0:T(128)S(1)} %iota_add_fusion.1, s32[96]{0:T(128)S(1)} %iota.43), dimensions={0}, to_apply=%region_2.3 | sort | flops 672 | bytes 1536 | tf_op jit(solution)/shard_map/jit(argsort)/sort | solution.py:32
  8.5 2.5 %sort.76 = (s32[96]{0:T(128)}, s32[96]{0:T(128)S(1)}) sort(s32[96]{0:T(128)S(1)} %dynamic_slice.22, s32[96]{0:T(128)S(1)} %iota.40), dimensions={0}, to_apply=%region_0.0 | sort | flops 672 | bytes 1536 | tf_op jit(solution)/shard_map/jit(argsort)/sort | solution.py:68
  12.4 4.6 %collective-permute-start.4 = (bf16[1,12,2560]{2,1,0:T(8,128)(2,1)S(1)}, bf16[1,12,2560]{2,1,0:T(8,128)(2,1)S(1)}, u32[]{:S(2)}, u32[]{:S(2)}) collective-permute-start(bf16[1,12,2560]{2,1,0:T(8,128)(2,1)S(1)} %get-tuple-element.93), channel_id=1, source_target_pairs={{0,28},{4,0},{8,4},{12,8},{16,12},{20,16},{24,20},{28,24},{1,29},{... | collective-permute-start | bytes 184328 | tf_op jit(solution)/shard_map/ppermute | solution.py:18
  17.6 2.7 %collective-permute-start.7 = (bf16[1,12,2560]{2,1,0:T(8,128)(2,1)S(1)}, bf16[1,12,2560]{2,1,0:T(8,128)(2,1)S(1)}, u32[]{:S(2)}, u32[]{:S(2)}) collective-permute-start(bf16[1,12,2560]{2,1,0:T(8,128)(2,1)S(1)} %get-tuple-element.90), channel_id=1, source_target_pairs={{0,16},{4,20},{8,24},{12,28},{16,0},{20,4},{24,8},{28,12},{1,17},{... | collective-permute-start | bytes 184328 | tf_op jit(solution)/shard_map/ppermute | solution.py:18
  22.1 4.7 %all-to-all-start.1 = ((bf16[8,12,2560]{2,1,0:T(8,128)(2,1)}), bf16[8,12,2560]{2,1,0:T(8,128)(2,1)S(1)}, u32[]{:S(2)}, u32[]{:S(2)}) async-start(bf16[8,12,2560]{2,1,0:T(8,128)(2,1)} %reshape.82), calls=%async_computation.1 | async-start | bytes 1310720 | tf_op jit(solution)/shard_map/all_to_all | solution.py:76
  26.8 2.5 %sort.79 = (s32[96]{0:T(128)}, s32[96]{0:T(128)S(1)}) sort(s32[96]{0:T(128)S(1)} %get-tuple-element.50, s32[96]{0:T(128)S(1)} %iota.44), dimensions={0}, to_apply=%region_3.4 | sort | flops 672 | bytes 1536 | tf_op jit(solution)/shard_map/jit(argsort)/sort | solution.py:73
  29.4 2.1 collective-permute-start.9
  31.7 13.2 %collective-permute-done.9 = bf16[1,12,2560]{2,1,0:T(8,128)(2,1)S(1)} collective-permute-done((bf16[1,12,2560]{2,1,0:T(8,128)(2,1)S(1)}, bf16[1,12,2560]{2,1,0:T(8,128)(2,1)S(1)}, u32[]{:S(2)}, u32[]{:S(2)}) %collective-permute-start.9) | collective-permute-done | bytes 61472 | tf_op jit(solution)/shard_map/ppermute | solution.py:18
  46.5 4.5 %collective-permute-start.11 = (bf16[96,2560]{1,0:T(8,128)(2,1)S(1)}, bf16[96,2560]{1,0:T(8,128)(2,1)S(1)}, u32[]{:S(2)}, u32[]{:S(2)}) collective-permute-start(bf16[96,2560]{1,0:T(8,128)(2,1)S(1)} %gather_fusion.5), channel_id=1, source_target_pairs={{0,8},{4,12},{8,16},{12,20},{16,24},{20,28},{1,9},{5,13},{9,17},{1... | collective-permute-start | bytes 1474568 | tf_op jit(solution)/shard_map/ppermute | solution.py:26
  51.2 2.5 %collective-permute-start.12 = (bf16[96,2560]{1,0:T(8,128)(2,1)S(1)}, bf16[96,2560]{1,0:T(8,128)(2,1)}, u32[]{:S(2)}, u32[]{:S(2)}) collective-permute-start(bf16[96,2560]{1,0:T(8,128)(2,1)S(1)} %gather_fusion.5), channel_id=1, source_target_pairs={{0,4},{4,8},{8,12},{12,16},{16,20},{20,24},{24,28},{1,5},{5,9},{9,... | collective-permute-start | bytes 1474568 | tf_op jit(solution)/shard_map/ppermute | solution.py:26
  56.0 1.3 collective-permute-start.13
  57.3 1.3 collective-permute-start.14
  58.6 4.0 %collective-permute-done.11 = bf16[96,2560]{1,0:T(8,128)(2,1)S(1)} collective-permute-done((bf16[96,2560]{1,0:T(8,128)(2,1)S(1)}, bf16[96,2560]{1,0:T(8,128)(2,1)S(1)}, u32[]{:S(2)}, u32[]{:S(2)}) %collective-permute-start.11) | collective-permute-done | bytes 491552 | tf_op jit(solution)/shard_map/ppermute | solution.py:26
  63.4 1.8 constant_dynamic-update-slice_fusion.15
  65.2 7.4 %all-to-all-start = ((bf16[8,12,2560]{2,1,0:T(8,128)(2,1)}), bf16[8,12,2560]{2,1,0:T(8,128)(2,1)S(1)}, u32[]{:S(2)}, u32[]{:S(2)}) async-start(bf16[8,12,2560]{2,1,0:T(8,128)(2,1)} %reshape.80), calls=%async_computation | async-start | bytes 1310720 | tf_op jit(solution)/shard_map/all_to_all | solution.py:75
  74.5 4.2 %collective-permute-start = (bf16[96,2560]{1,0:T(8,128)(2,1)S(1)}, bf16[96,2560]{1,0:T(8,128)(2,1)S(1)}, u32[]{:S(2)}, u32[]{:S(2)}) collective-permute-start(bf16[96,2560]{1,0:T(8,128)(2,1)S(1)} %gather_fusion.3), channel_id=1, source_target_pairs={{0,8},{4,12},{8,16},{12,20},{16,24},{20,28},{1,9},{5,13},{9,17},{1... | collective-permute-start | bytes 1474568 | tf_op jit(solution)/shard_map/ppermute | solution.py:26
  78.6 1.8 constant_dynamic-update-slice_fusion.13
  80.5 2.3 %collective-permute-start.1 = (bf16[96,2560]{1,0:T(8,128)(2,1)S(1)}, bf16[96,2560]{1,0:T(8,128)(2,1)}, u32[]{:S(2)}, u32[]{:S(2)}) collective-permute-start(bf16[96,2560]{1,0:T(8,128)(2,1)S(1)} %gather_fusion.3), channel_id=1, source_target_pairs={{0,4},{4,8},{8,12},{12,16},{16,20},{20,24},{24,28},{1,5},{5,9},{9,... | collective-permute-start | bytes 1474568 | tf_op jit(solution)/shard_map/ppermute | solution.py:26
  83.3 1.9 constant_dynamic-update-slice_fusion.12
  85.2 1.3 collective-permute-start.2
  86.4 1.3 collective-permute-start.3
  87.7 4.6 %all-to-all-done = bf16[8,12,2560]{2,1,0:T(8,128)(2,1)S(1)} async-done(((bf16[8,12,2560]{2,1,0:T(8,128)(2,1)}), bf16[8,12,2560]{2,1,0:T(8,128)(2,1)S(1)}, u32[]{:S(2)}, u32[]{:S(2)}) %all-to-all-start) | async-done | bytes 491552 | tf_op jit(solution)/shard_map/all_to_all | solution.py:75
  93.4 1.7 collective-permute-done
  97.3 10.9 %collective-permute-done.3 = bf16[96,2560]{1,0:T(8,128)(2,1)} collective-permute-done((bf16[96,2560]{1,0:T(8,128)(2,1)S(1)}, bf16[96,2560]{1,0:T(8,128)(2,1)}, u32[]{:S(2)}, u32[]{:S(2)}) %collective-permute-start.3) | collective-permute-done | bytes 491552 | tf_op jit(solution)/shard_map/ppermute | solution.py:26
  109.3 1.4 copy-done.3
  110.7 79.9 %while.11 = (s32[]{:T(128)}, bf16[20,96,128]{2,1,0:T(8,128)(2,1)S(1)}, s32[20]{0:T(128)S(1)}, bf16[96,2560]{1,0:T(8,128)(2,1)S(1)}, bf16[480,2560]{1,0:T(8,128)(...) while((s32[]{:T(128)}, ...), condition=%wide.region_8.10_spmd.clone, body=%wide.region_5.9_spmd.clone.sunk | while | flops 23973700 | bytes 1052395 | solution.py:55
  116.1 1.2 fusion.23
  120.1 1.2 fusion.23
  124.1 1.2 fusion.23
  128.1 1.2 fusion.23
  132.1 1.2 fusion.23
  136.1 1.2 fusion.23
  140.1 1.2 fusion.23
  144.1 1.2 fusion.23
  148.1 1.2 fusion.23
  152.1 1.2 fusion.23
  156.1 1.2 fusion.23
  164.1 1.2 fusion.23
  168.1 1.2 fusion.23
  172.1 1.2 fusion.23
  180.1 1.2 fusion.23
  184.1 1.2 fusion.23
  188.1 1.2 fusion.23
  192.5 3.5 %all-to-all-start.2 = ((bf16[8,12,2560]{2,1,0:T(8,128)(2,1)}), bf16[8,12,2560]{2,1,0:T(8,128)(2,1)S(1)}, u32[]{:S(2)}, u32[]{:S(2)}) async-start(bf16[8,12,2560]{2,1,0:T(8,128)(2,1)} %reshape.89), calls=%async_computation.2 | async-start | bytes 1310720 | tf_op jit(solution)/shard_map/all_to_all | solution.py:100
  196.1 2.5 %sort.80 = (s32[96]{0:T(128)}, s32[96]{0:T(128)S(1)}) sort(s32[96]{0:T(128)S(1)} %get-tuple-element.48, s32[96]{0:T(128)S(1)} %iota.46), dimensions={0}, to_apply=%region_9.11 | sort | flops 672 | bytes 1536 | tf_op jit(solution)/shard_map/jit(argsort)/sort | solution.py:101
  198.6 15.5 %all-to-all-done.2 = bf16[8,12,2560]{2,1,0:T(8,128)(2,1)S(1)} async-done(((bf16[8,12,2560]{2,1,0:T(8,128)(2,1)}), bf16[8,12,2560]{2,1,0:T(8,128)(2,1)S(1)}, u32[]{:S(2)}, u32[]{:S(2)}) %all-to-all-start.2) | async-done | bytes 491552 | tf_op jit(solution)/shard_map/all_to_all | solution.py:100
  214.2 1.6 gather_fusion.7
  (190 shorter events, 63.6 us)
Async XLA Ops:
  0.0 11.1 %copy-start = (bf16[96,2560]{1,0:T(8,128)(2,1)S(1)}, bf16[96,2560]{1,0:T(8,128)(2,1)}, u32[]{:S(2)}) copy-start(bf16[96,2560]{1,0:T(8,128)(2,1)} %param.12) | copy-start | bytes 1474564
  11.9 8.4 %copy-start.1 = (bf16[96,2560]{1,0:T(8,128)(2,1)S(1)}, bf16[96,2560]{1,0:T(8,128)(2,1)}, u32[]{:S(2)}) copy-start(bf16[96,2560]{1,0:T(8,128)(2,1)} %param.11) | copy-start | bytes 1474564
  12.4 17.0 %collective-permute-start.4 = (bf16[1,12,2560]{2,1,0:T(8,128)(2,1)S(1)}, bf16[1,12,2560]{2,1,0:T(8,128)(2,1)S(1)}, u32[]{:S(2)}, u32[]{:S(2)}) collective-permute-start(bf16[1,12,2560]{2,1,0:T(8,128)(2,1)S(1)} %get-tuple-element.93), channel_id=1, source_target_pairs={{0,28},{4,0},{8,4},{12,8},{16,12},{20,16},{24,20},{28,24},{1,29},{... | collective-permute-start | bytes 184328 | tf_op jit(solution)/shard_map/ppermute | solution.py:18
  17.0 14.5 %collective-permute-start.5 = (bf16[1,12,2560]{2,1,0:T(8,128)(2,1)S(1)}, bf16[1,12,2560]{2,1,0:T(8,128)(2,1)S(1)}, u32[]{:S(2)}, u32[]{:S(2)}) collective-permute-start(bf16[1,12,2560]{2,1,0:T(8,128)(2,1)S(1)} %get-tuple-element.92), channel_id=1, source_target_pairs={{0,24},{4,28},{8,0},{12,4},{16,8},{20,12},{24,16},{28,20},{1,25},{... | collective-permute-start | bytes 184328 | tf_op jit(solution)/shard_map/ppermute | solution.py:18
  17.6 14.0 %collective-permute-start.6 = (bf16[1,12,2560]{2,1,0:T(8,128)(2,1)S(1)}, bf16[1,12,2560]{2,1,0:T(8,128)(2,1)S(1)}, u32[]{:S(2)}, u32[]{:S(2)}) collective-permute-start(bf16[1,12,2560]{2,1,0:T(8,128)(2,1)S(1)} %get-tuple-element.91), channel_id=1, source_target_pairs={{0,20},{4,24},{8,28},{12,0},{16,4},{20,8},{24,12},{28,16},{1,21},{... | collective-permute-start | bytes 184328 | tf_op jit(solution)/shard_map/ppermute | solution.py:18
  17.6 14.0 %collective-permute-start.7 = (bf16[1,12,2560]{2,1,0:T(8,128)(2,1)S(1)}, bf16[1,12,2560]{2,1,0:T(8,128)(2,1)S(1)}, u32[]{:S(2)}, u32[]{:S(2)}) collective-permute-start(bf16[1,12,2560]{2,1,0:T(8,128)(2,1)S(1)} %get-tuple-element.90), channel_id=1, source_target_pairs={{0,16},{4,20},{8,24},{12,28},{16,0},{20,4},{24,8},{28,12},{1,17},{... | collective-permute-start | bytes 184328 | tf_op jit(solution)/shard_map/ppermute | solution.py:18
  20.3 11.3 %collective-permute-start.8 = (bf16[1,12,2560]{2,1,0:T(8,128)(2,1)S(1)}, bf16[1,12,2560]{2,1,0:T(8,128)(2,1)S(1)}, u32[]{:S(2)}, u32[]{:S(2)}) collective-permute-start(bf16[1,12,2560]{2,1,0:T(8,128)(2,1)S(1)} %get-tuple-element.89), channel_id=1, source_target_pairs={{0,12},{4,16},{8,20},{12,24},{16,28},{20,0},{24,4},{28,8},{1,13},{... | collective-permute-start | bytes 184328 | tf_op jit(solution)/shard_map/ppermute | solution.py:18
  22.1 43.1 %all-to-all-start.1 = ((bf16[8,12,2560]{2,1,0:T(8,128)(2,1)}), bf16[8,12,2560]{2,1,0:T(8,128)(2,1)S(1)}, u32[]{:S(2)}, u32[]{:S(2)}) async-start(bf16[8,12,2560]{2,1,0:T(8,128)(2,1)} %reshape.82), calls=%async_computation.1 | async-start | bytes 1310720 | tf_op jit(solution)/shard_map/all_to_all | solution.py:76
  29.4 15.4 %collective-permute-start.9 = (bf16[1,12,2560]{2,1,0:T(8,128)(2,1)S(1)}, bf16[1,12,2560]{2,1,0:T(8,128)(2,1)S(1)}, u32[]{:S(2)}, u32[]{:S(2)}) collective-permute-start(bf16[1,12,2560]{2,1,0:T(8,128)(2,1)S(1)} %get-tuple-element.88), channel_id=1, source_target_pairs={{0,8},{4,12},{8,16},{12,20},{16,24},{20,28},{24,0},{28,4},{1,9},{5... | collective-permute-start | bytes 184328 | tf_op jit(solution)/shard_map/ppermute | solution.py:18
  31.5 13.6 %collective-permute-start.10 = (bf16[1,12,2560]{2,1,0:T(8,128)(2,1)S(1)}, bf16[1,12,2560]{2,1,0:T(8,128)(2,1)S(1)}, u32[]{:S(2)}, u32[]{:S(2)}) collective-permute-start(bf16[1,12,2560]{2,1,0:T(8,128)(2,1)S(1)} %get-tuple-element.87), channel_id=1, source_target_pairs={{0,4},{4,8},{8,12},{12,16},{16,20},{20,24},{24,28},{28,0},{1,5},{5... | collective-permute-start | bytes 184328 | tf_op jit(solution)/shard_map/ppermute | solution.py:18
  45.6 5.6 %copy-start.6 = (s32[2]{0:T(128)S(1)}, s32[2]{0:T(128)}, u32[]{:S(2)}) copy-start(s32[2]{0:T(128)} %param.15) | copy-start | bytes 28
  45.6 8.1 %copy-start.5 = (s32[2,4]{1,0:T(2,128)S(1)}, s32[2,4]{1,0:T(2,128)}, u32[]{:S(2)}) copy-start(s32[2,4]{1,0:T(2,128)} %param.14) | copy-start | bytes 100
  45.6 8.2 %copy-start.2 = (bf16[96,2560]{1,0:T(8,128)(2,1)S(1)}, bf16[96,2560]{1,0:T(8,128)(2,1)}, u32[]{:S(2)}) copy-start(bf16[96,2560]{1,0:T(8,128)(2,1)} %param.10) | copy-start | bytes 1474564
  46.5 16.1 %collective-permute-start.11 = (bf16[96,2560]{1,0:T(8,128)(2,1)S(1)}, bf16[96,2560]{1,0:T(8,128)(2,1)S(1)}, u32[]{:S(2)}, u32[]{:S(2)}) collective-permute-start(bf16[96,2560]{1,0:T(8,128)(2,1)S(1)} %gather_fusion.5), channel_id=1, source_target_pairs={{0,8},{4,12},{8,16},{12,20},{16,24},{20,28},{1,9},{5,13},{9,17},{1... | collective-permute-start | bytes 1474568 | tf_op jit(solution)/shard_map/ppermute | solution.py:26
  51.2 12.2 %collective-permute-start.12 = (bf16[96,2560]{1,0:T(8,128)(2,1)S(1)}, bf16[96,2560]{1,0:T(8,128)(2,1)}, u32[]{:S(2)}, u32[]{:S(2)}) collective-permute-start(bf16[96,2560]{1,0:T(8,128)(2,1)S(1)} %gather_fusion.5), channel_id=1, source_target_pairs={{0,4},{4,8},{8,12},{12,16},{16,20},{20,24},{24,28},{1,5},{5,9},{9,... | collective-permute-start | bytes 1474568 | tf_op jit(solution)/shard_map/ppermute | solution.py:26
  56.0 22.7 %collective-permute-start.13 = (bf16[96,2560]{1,0:T(8,128)(2,1)S(1)}, bf16[96,2560]{1,0:T(8,128)(2,1)}, u32[]{:S(2)}, u32[]{:S(2)}) collective-permute-start(bf16[96,2560]{1,0:T(8,128)(2,1)S(1)} %gather_fusion.5), channel_id=1, source_target_pairs={{4,0},{8,4},{12,8},{16,12},{20,16},{24,20},{28,24},{5,1},{9,5},{13... | collective-permute-start | bytes 1474568 | tf_op jit(solution)/shard_map/ppermute | solution.py:26
  57.3 26.0 %collective-permute-start.14 = (bf16[96,2560]{1,0:T(8,128)(2,1)S(1)}, bf16[96,2560]{1,0:T(8,128)(2,1)}, u32[]{:S(2)}, u32[]{:S(2)}) collective-permute-start(bf16[96,2560]{1,0:T(8,128)(2,1)S(1)} %gather_fusion.5), channel_id=1, source_target_pairs={{8,0},{12,4},{16,8},{20,12},{24,16},{28,20},{9,1},{13,5},{17,9},{2... | collective-permute-start | bytes 1474568 | tf_op jit(solution)/shard_map/ppermute | solution.py:26
  65.2 27.2 %all-to-all-start = ((bf16[8,12,2560]{2,1,0:T(8,128)(2,1)}), bf16[8,12,2560]{2,1,0:T(8,128)(2,1)S(1)}, u32[]{:S(2)}, u32[]{:S(2)}) async-start(bf16[8,12,2560]{2,1,0:T(8,128)(2,1)} %reshape.80), calls=%async_computation | async-start | bytes 1310720 | tf_op jit(solution)/shard_map/all_to_all | solution.py:75
  74.5 20.6 %collective-permute-start = (bf16[96,2560]{1,0:T(8,128)(2,1)S(1)}, bf16[96,2560]{1,0:T(8,128)(2,1)S(1)}, u32[]{:S(2)}, u32[]{:S(2)}) collective-permute-start(bf16[96,2560]{1,0:T(8,128)(2,1)S(1)} %gather_fusion.3), channel_id=1, source_target_pairs={{0,8},{4,12},{8,16},{12,20},{16,24},{20,28},{1,9},{5,13},{9,17},{1... | collective-permute-start | bytes 1474568 | tf_op jit(solution)/shard_map/ppermute | solution.py:26
  80.5 14.6 %collective-permute-start.1 = (bf16[96,2560]{1,0:T(8,128)(2,1)S(1)}, bf16[96,2560]{1,0:T(8,128)(2,1)}, u32[]{:S(2)}, u32[]{:S(2)}) collective-permute-start(bf16[96,2560]{1,0:T(8,128)(2,1)S(1)} %gather_fusion.3), channel_id=1, source_target_pairs={{0,4},{4,8},{8,12},{12,16},{16,20},{20,24},{24,28},{1,5},{5,9},{9,... | collective-permute-start | bytes 1474568 | tf_op jit(solution)/shard_map/ppermute | solution.py:26
  85.2 11.0 %collective-permute-start.2 = (bf16[96,2560]{1,0:T(8,128)(2,1)S(1)}, bf16[96,2560]{1,0:T(8,128)(2,1)}, u32[]{:S(2)}, u32[]{:S(2)}) collective-permute-start(bf16[96,2560]{1,0:T(8,128)(2,1)S(1)} %gather_fusion.3), channel_id=1, source_target_pairs={{4,0},{8,4},{12,8},{16,12},{20,16},{24,20},{28,24},{5,1},{9,5},{13... | collective-permute-start | bytes 1474568 | tf_op jit(solution)/shard_map/ppermute | solution.py:26
  86.4 21.7 %collective-permute-start.3 = (bf16[96,2560]{1,0:T(8,128)(2,1)S(1)}, bf16[96,2560]{1,0:T(8,128)(2,1)}, u32[]{:S(2)}, u32[]{:S(2)}) collective-permute-start(bf16[96,2560]{1,0:T(8,128)(2,1)S(1)} %gather_fusion.3), channel_id=1, source_target_pairs={{8,0},{12,4},{16,8},{20,12},{24,16},{28,20},{9,1},{13,5},{17,9},{2... | collective-permute-start | bytes 1474568 | tf_op jit(solution)/shard_map/ppermute | solution.py:26
  93.4 17.3 %copy-start.4 = (bf16[20,96,128]{2,1,0:T(8,128)(2,1)S(1)}, bf16[20,96,128]{2,1,0:T(8,128)(2,1)}, u32[]{:S(2)}) copy-start(bf16[20,96,128]{2,1,0:T(8,128)(2,1)} %custom-call.19) | copy-start | bytes 1474564
  109.3 1.4 copy-start.3
  192.5 21.6 %all-to-all-start.2 = ((bf16[8,12,2560]{2,1,0:T(8,128)(2,1)}), bf16[8,12,2560]{2,1,0:T(8,128)(2,1)S(1)}, u32[]{:S(2)}, u32[]{:S(2)}) async-start(bf16[8,12,2560]{2,1,0:T(8,128)(2,1)} %reshape.89), calls=%async_computation.2 | async-start | bytes 1310720 | tf_op jit(solution)/shard_map/all_to_all | solution.py:100
